TPU v7x, 512 devices: a whole 4x4x16 slice. The times are simulated.
512 devices in a mesh: ctx: 32 (over x, y, core), head: 16 (over z).
Axes of the slice: x: 4, y: 4, z: 16, core: 2. Of those that a mesh axis runs over, the one named last changes fastest.
Arguments:
- mixed_in: bfloat16 [8192, 8192], P(('ctx', 'head')), may hold values from -6 to 6
- conv_weight: float32 [4, 8192], P(None, 'head'), may hold values from -3 to 3
- write_strength_logit: float32 [32, 8192], P('head', 'ctx'), may hold values from -10.5 to 2.2, as said below
- decay_log: float32 [32, 8192], P('head', 'ctx'), may hold values from -0.7 to 0, as said below
- initial_state: float32 [32, 128, 128], P('head'), may hold values from -6 to 6
- final_state_grad: float32 [32, 128, 128], P('head'), may hold values from -6 to 6
- grad_out: bfloat16 [8192, 4096], P('ctx', 'head'), may hold values from -6 to 6
Outputs:
- grad_mixed: bfloat16 [8192, 8192], P(('ctx', 'head'))
- grad_conv: float32 [4, 8192], P(None, 'head')
- grad_beta_logit: float32 [32, 8192], P('head', 'ctx')
- grad_decay_log: float32 [32, 8192], P('head', 'ctx')
Inputs may be any that keep to these rules, and one draw needn't show every extreme that they name: `write_strength_logit`: each value head's write strengths and decays vary from token to token. `decay_log`: every entry is negative.
All inputs are finite; a program needn't handle non-finite values.
Results may differ from a plain program's by a relative error of at most 0.001.
Values may be sent and summed in bfloat16 or wider, within the bound.
A program may use at most 64 MiB of HBM per device.

v0:
```python
import jax
import jax.numpy as jnp
from jax import lax
from jax.sharding import PartitionSpec as P

HK = 16
VALUE_HEADS = 32
DK = 128
DV = 128
KW = 4
BLOCK = 64
highest = lax.Precision.HIGHEST
norm_eps = 1e-06


def from_behind(value, axis, by):
    devices = lax.axis_size(axis)
    pairs = [(i, i + by) for i in range(devices) if 0 <= i + by < devices]
    return lax.ppermute(value, axis, pairs)


def prefix(value, axis, combine, identity, reverse):
    devices, mine = (lax.axis_size(axis), lax.axis_index(axis))
    everything = jax.tree.map(lambda part: lax.all_gather(part, axis), value)
    start = jax.tree.map(
        lambda part, zero: jnp.broadcast_to(jnp.asarray(zero, part.dtype), part.shape),
        value,
        identity,
    )

    def step(k, before):
        at = devices - 1 - k if reverse else k
        reached = at > mine if reverse else at < mine
        new = combine(before, jax.tree.map(lambda part: part[at], everything))
        return jax.tree.map(lambda a, b: jnp.where(reached, a, b), new, before)

    return lax.fori_loop(0, devices, step, start)


def block_step(carried, pieces):
    state, transit = carried
    queries, key_feats, values, beta_gate, log_decay = pieces
    block_size = log_decay.shape[0]
    cumulative = jnp.cumsum(log_decay)
    row_ids = lax.broadcasted_iota(jnp.int32, (block_size, block_size), 0)
    col_ids = lax.broadcasted_iota(jnp.int32, (block_size, block_size), 1)
    causal = col_ids <= row_ids
    differ = jnp.where(causal, cumulative[:, None] - cumulative[None, :], 0.0)
    ratios = jnp.where(causal, jnp.exp(differ), 0.0)
    key_gram = jnp.dot(key_feats, key_feats.T, precision=highest)
    lower_part = jnp.where(col_ids < row_ids, beta_gate[:, None] * ratios * key_gram, 0.0)
    system = lower_part + jnp.eye(block_size, dtype=jnp.float32)
    decays = jnp.exp(cumulative)
    right_sides = jnp.concatenate(
        [beta_gate[:, None] * values, (beta_gate * decays)[:, None] * key_feats], axis=1
    )
    solved = jax.scipy.linalg.solve_triangular(system, right_sides, lower=True)
    width_v = values.shape[1]
    base_update = solved[:, :width_v]
    weights = solved[:, width_v:]
    update = base_update - jnp.dot(weights, state, precision=highest)
    scores = ratios * jnp.dot(queries, key_feats.T, precision=highest)
    output = decays[:, None] * jnp.dot(queries, state, precision=highest) + jnp.dot(
        scores, update, precision=highest
    )
    total_decay = jnp.exp(cumulative[-1])
    tail_keys = jnp.exp(cumulative[-1] - cumulative)[:, None] * key_feats
    new_state = total_decay * state + jnp.dot(tail_keys.T, update, precision=highest)
    step_map = total_decay * jnp.eye(key_feats.shape[1], dtype=jnp.float32) - jnp.dot(
        tail_keys.T, weights, precision=highest
    )
    new_transit = jnp.dot(step_map, transit, precision=highest)
    return ((new_state, new_transit), output)


def run_head(state, queries, key_feats, values, beta_gate, log_decay):
    blocks = queries.shape[0] // BLOCK
    pieces = (
        queries.reshape(blocks, BLOCK, -1),
        key_feats.reshape(blocks, BLOCK, -1),
        values.reshape(blocks, BLOCK, -1),
        beta_gate.reshape(blocks, BLOCK),
        log_decay.reshape(blocks, BLOCK),
    )
    start = (state, jnp.eye(key_feats.shape[1], dtype=jnp.float32))
    (state_end, transit), outputs = lax.scan(block_step, start, pieces)
    return (outputs.reshape(-1, values.shape[1]), state_end, transit)


def normalize(feats, factor):
    return feats * lax.rsqrt(jnp.sum(feats * feats, axis=-1, keepdims=True) + norm_eps) * factor


def mix_layer(state_in, extended, conv_weight, write_strength_logit, decay_log):
    row_count = extended.shape[0] - (KW - 1)
    filtered_signal = conv_weight[0] * extended[0:row_count]
    for tap in range(1, KW):
        filtered_signal = filtered_signal + conv_weight[tap] * extended[tap : tap + row_count]
    activated = jax.nn.silu(filtered_signal)
    ratio_heads = VALUE_HEADS // HK
    group_width = 2 * DK + ratio_heads * DV
    groups = activated.reshape(row_count, -1, group_width)
    key_heads = groups.shape[1]
    queries = normalize(groups[:, :, :DK], DK ** (-0.5))
    key_feats = normalize(groups[:, :, DK : 2 * DK], 1.0)
    values = (
        groups[:, :, 2 * DK :].reshape(row_count, key_heads * ratio_heads, DV).transpose(1, 0, 2)
    )
    queries = jnp.repeat(queries.transpose(1, 0, 2), ratio_heads, axis=0)
    key_feats = jnp.repeat(key_feats.transpose(1, 0, 2), ratio_heads, axis=0)
    beta_gate = jax.nn.sigmoid(write_strength_logit)
    outputs, state_out, transit = jax.vmap(run_head)(
        state_in, queries, key_feats, values, beta_gate, decay_log
    )
    result = outputs.transpose(1, 0, 2).reshape(row_count, -1)
    return ((result, state_out), transit)


def compose(earlier, later):
    matrix = jnp.einsum("hij,hjk->hik", later[0], earlier[0], precision=highest)
    offset = jnp.einsum("hij,hjk->hik", later[0], earlier[1], precision=highest) + later[1]
    return (matrix, offset)


def advance(maps, state):
    return jnp.einsum("hij,hjk->hik", maps[0], state, precision=highest) + maps[1]


def on_device(
    mixed_in,
    conv_weight,
    write_strength_logit,
    decay_log,
    initial_state,
    final_state_grad,
    grad_out,
):
    local_in = lax.all_to_all(mixed_in, "head", split_axis=1, concat_axis=0, tiled=True)
    edge_rows = from_behind(local_in[-(KW - 1) :], "ctx", 1)
    extended = jnp.concatenate([edge_rows, local_in], axis=0).astype(jnp.float32)
    cotangent = grad_out.astype(jnp.float32)
    zeros_state = jnp.zeros_like(initial_state)

    def from_state(state):
        return mix_layer(state, extended, conv_weight, write_strength_logit, decay_log)

    primal, pull_state, transit = jax.vjp(from_state, zeros_state, has_aux=True)
    offset = primal[1]
    local_grad = pull_state((cotangent, jnp.zeros_like(offset)))[0]
    flipped = jnp.swapaxes(transit, 1, 2)
    identity = (
        jnp.broadcast_to(jnp.eye(transit.shape[1], dtype=jnp.float32), transit.shape),
        jnp.zeros_like(offset),
    )
    earlier_map = prefix((transit, offset), "ctx", compose, identity, False)
    later_map = prefix((flipped, local_grad), "ctx", compose, identity, True)
    state_in = advance(earlier_map, initial_state)
    state_grad = advance(later_map, final_state_grad)

    def forward(ext_rows, weight_taps, logits, decay_logs):
        return mix_layer(state_in, ext_rows, weight_taps, logits, decay_logs)

    unused, pull_all, unused_transit = jax.vjp(
        forward, extended, conv_weight, write_strength_logit, decay_log, has_aux=True
    )
    grad_ext, grad_weight, grad_beta, grad_decay = pull_all((cotangent, state_grad))
    spilled = from_behind(grad_ext[: KW - 1], "ctx", -1)
    own_grad = grad_ext[KW - 1 :]
    own_grad = jnp.concatenate([own_grad[: -(KW - 1)], own_grad[-(KW - 1) :] + spilled], axis=0)
    returned = lax.all_to_all(
        own_grad.astype(jnp.bfloat16), "head", split_axis=0, concat_axis=1, tiled=True
    )
    weight_total = lax.psum(grad_weight, "ctx")
    return (returned, weight_total, grad_beta, grad_decay)


def solution(mesh):
    in_specs = (
        P(("ctx", "head"), None),
        P(None, "head"),
        P("head", "ctx"),
        P("head", "ctx"),
        P("head", None, None),
        P("head", None, None),
        P("ctx", "head"),
    )
    out_specs = (P(("ctx", "head"), None), P(None, "head"), P("head", "ctx"), P("head", "ctx"))
    return jax.shard_map(
        on_device, mesh=mesh, in_specs=in_specs, out_specs=out_specs, check_vma=False
    )
```

profile of v0, /device:TPU:32, one launch (start us, length us, event | category | flops | bytes accessed | tf_op | source)
XLA Modules:
  0.0 795.1 jit_solution(5155768118002871086)
XLA Ops:
  7.2 1.7 copy.147
  8.9 15.2 %all-to-all-start = ((bf16[16,16,512]{2,0,1:T(8,128)(2,1)}), bf16[16,16,512]{2,0,1:T(8,128)(2,1)S(1)}, u32[]{:S(2)}, u32[]{:S(2)}) async-start(bf16[16,16,512]{2,0,1:T(8,128)(2,1)} %bitcast.435), calls=%async_computation | async-start | bytes 524288 | tf_op jit(solution)/shard_map/all_to_all | solution.py:138
  26.4 15.6 %all-to-all-done = bf16[16,16,512]{2,0,1:T(8,128)(2,1)S(1)} async-done(((bf16[16,16,512]{2,0,1:T(8,128)(2,1)}), bf16[16,16,512]{2,0,1:T(8,128)(2,1)S(1)}, u32[]{:S(2)}, u32[]{:S(2)}) %all-to-all-start) | async-done | bytes 262176 | tf_op jit(solution)/shard_map/all_to_all | solution.py:138
  48.5 65.6 %while.169 = (s32[]{:T(128)}, f32[2,128,128]{2,1,0:T(8,128)S(1)}, f32[2,128,128]{2,1,0:T(8,128)S(1)}, f32[4,2,64,128]{3,2,1,0:T(8,128)S(1)}, f32[4,2,64,1]{2,1,3...) while((s32[]{:T(128)}, f32[2,128,128]{2,1,0:T(8,128)S(1)}, ...), condition=%wide.region_4.6_spmd.clone.clone, body=%wide.region_2.5_spmd.clone.clone.sunk | while | flops 176640128 | bytes 2980628 | solution.py:86
  51.5 9.8 %custom-call.35 = f32[2,1,64,64]{2,3,1,0:T(8,128)S(1)} custom-call(f32[2,1,64,64]{3,2,1,0:T(8,128)S(1)} %fusion.420), custom_call_target="InvertDiagBlocksLowerTriangular" | custom-call | tf_op jit(solution)/shard_map/jvp(vmap())/while/body/eval_jaxpr/jit(_solve_triangular)/triangular_solve/custom-call.1 | solution.py:57
  67.9 9.8 %custom-call.35 = f32[2,1,64,64]{2,3,1,0:T(8,128)S(1)} custom-call(f32[2,1,64,64]{3,2,1,0:T(8,128)S(1)} %fusion.420), custom_call_target="InvertDiagBlocksLowerTriangular" | custom-call | tf_op jit(solution)/shard_map/jvp(vmap())/while/body/eval_jaxpr/jit(_solve_triangular)/triangular_solve/custom-call.1 | solution.py:57
  84.2 9.8 %custom-call.35 = f32[2,1,64,64]{2,3,1,0:T(8,128)S(1)} custom-call(f32[2,1,64,64]{3,2,1,0:T(8,128)S(1)} %fusion.420), custom_call_target="InvertDiagBlocksLowerTriangular" | custom-call | tf_op jit(solution)/shard_map/jvp(vmap())/while/body/eval_jaxpr/jit(_solve_triangular)/triangular_solve/custom-call.1 | solution.py:57
  100.7 9.8 %custom-call.35 = f32[2,1,64,64]{2,3,1,0:T(8,128)S(1)} custom-call(f32[2,1,64,64]{3,2,1,0:T(8,128)S(1)} %fusion.420), custom_call_target="InvertDiagBlocksLowerTriangular" | custom-call | tf_op jit(solution)/shard_map/jvp(vmap())/while/body/eval_jaxpr/jit(_solve_triangular)/triangular_solve/custom-call.1 | solution.py:57
  116.9 9.2 %while.166 = (s32[]{:T(128)}, f32[2,128,128]{2,1,0:T(8,128)S(1)}, f32[4,2,1,1]{1,3,2,0:T(1,128)S(1)}, f32[4,2,64,128]{3,2,1,0:T(8,128)S(1)}, f32[4,2,64,1]{2,1,3...) while((s32[]{:T(128)}, f32[2,128,128]{2,1,0:T(8,128)S(1)}, ...), condition=%wide.region_6.8_spmd.clone, body=%wide.region_5.7_spmd.clone.sunk | while | flops 88293376 | bytes 1316019 | solution.py:86
  128.2 45.1 %all-gather.9.cloned.1.call-done = f32[64,128,128]{2,1,0:T(8,128)} async-done(((f32[2,128,128]{2,1,0:T(8,128)}), f32[64,128,128]{2,1,0:T(8,128)}) %all-gather.9.cloned.1.call-update) | async-done | bytes 4194320 | tf_op jit(solution)/shard_map/all_gather | solution.py:24
  173.2 64.6 %all-gather.11.cloned.1.call-done = f32[64,128,128]{2,1,0:T(8,128)} async-done(((f32[2,128,128]{2,1,0:T(8,128)}), f32[64,128,128]{2,1,0:T(8,128)}) %all-gather.11.cloned.1.call-update) | async-done | bytes 4194320 | tf_op jit(solution)/shard_map/all_gather | solution.py:24
  237.9 80.1 %while.167 = (s32[]{:T(128)}, f32[2,128,128]{2,1,0:T(8,128)S(1)}, f32[2,128,128]{2,1,0:T(8,128)S(1)}, s32[]{:T(128)}, f32[32,2,128,128]{3,2,1,0:T(8,128)}, /*ind...) while((s32[]{:T(128)}, f32[2,128,128]{2,1,0:T(8,128)S(1)}, ...), condition=%wide.region_8.10_spmd.clone, body=%wide.region_7.9_spmd.clone.sunk | while | flops 100827144 | bytes 1706674 | solution.py:37
  318.0 47.8 %all-gather.15.cloned.1.call-done = f32[64,128,128]{2,1,0:T(8,128)} async-done(((f32[2,128,128]{2,1,0:T(8,128)}), f32[64,128,128]{2,1,0:T(8,128)}) %all-gather.15.cloned.1.call-update) | async-done | bytes 4194320 | tf_op jit(solution)/shard_map/all_gather | solution.py:24
  365.9 79.6 %while.168 = (s32[]{:T(128)}, f32[2,128,128]{2,1,0:T(8,128)S(1)}, f32[2,128,128]{2,1,0:T(8,128)S(1)}, s32[]{:T(128)}, f32[32,2,128,128]{3,2,1,0:T(8,128)}, /*ind...) while((s32[]{:T(128)}, f32[2,128,128]{2,1,0:T(8,128)S(1)}, f32[2,128,128]{2,1,0:T(8,128)S(1)}, ...), condition=%wide.region_10.12_spmd.clone, body=%wide.region_9.11_spmd.clone.sunk | while | flops 100827136 | bytes 1706612 | solution.py:37
  458.0 107.3 %while.164 = (s32[]{:T(128)}, f32[2,128,128]{2,1,0:T(8,128)S(1)}, f32[4,2,64,64]{3,2,1,0:T(8,128)}, f32[4,2,128,64]{2,3,1,0:T(8,128)}, f32[4,2,64,64]{3,2,1,0:T(...) while((s32[]{:T(128)}, f32[2,128,128]{2,1,0:T(8,128)S(1)}, ...), condition=%wide.region_13.15_spmd.clone.clone, body=%wide.region_11.14_spmd.clone.clone.sunk | while | flops 126194176 | bytes 3312057 | solution.py:86
  461.6 1.4 select_bitcast_fusion.4
  463.0 11.2 %custom-call.33 = f32[2,1,64,64]{2,3,1,0:T(8,128)} custom-call(f32[2,1,64,64]{3,2,1,0:T(8,128)} %select_bitcast_fusion.4), custom_call_target="InvertDiagBlocksLowerTriangular" | custom-call | tf_op jit(solution)/shard_map/jvp(vmap())/while/body/eval_jaxpr/jit(_solve_triangular)/triangular_solve/custom-call.1 | solution.py:57
  474.2 1.8 bitcast_dynamic-update-slice_fusion.22
  477.4 1.7 bitcast_dynamic-update-slice_fusion.24
  488.4 1.4 select_bitcast_fusion.4
  489.8 11.2 %custom-call.33 = f32[2,1,64,64]{2,3,1,0:T(8,128)} custom-call(f32[2,1,64,64]{3,2,1,0:T(8,128)} %select_bitcast_fusion.4), custom_call_target="InvertDiagBlocksLowerTriangular" | custom-call | tf_op jit(solution)/shard_map/jvp(vmap())/while/body/eval_jaxpr/jit(_solve_triangular)/triangular_solve/custom-call.1 | solution.py:57
  501.0 1.8 bitcast_dynamic-update-slice_fusion.22
  504.2 1.7 bitcast_dynamic-update-slice_fusion.24
  515.2 1.4 select_bitcast_fusion.4
  516.6 11.2 %custom-call.33 = f32[2,1,64,64]{2,3,1,0:T(8,128)} custom-call(f32[2,1,64,64]{3,2,1,0:T(8,128)} %select_bitcast_fusion.4), custom_call_target="InvertDiagBlocksLowerTriangular" | custom-call | tf_op jit(solution)/shard_map/jvp(vmap())/while/body/eval_jaxpr/jit(_solve_triangular)/triangular_solve/custom-call.1 | solution.py:57
  527.8 1.8 bitcast_dynamic-update-slice_fusion.22
  531.0 1.7 bitcast_dynamic-update-slice_fusion.24
  542.1 1.4 select_bitcast_fusion.4
  543.5 11.2 %custom-call.33 = f32[2,1,64,64]{2,3,1,0:T(8,128)} custom-call(f32[2,1,64,64]{3,2,1,0:T(8,128)} %select_bitcast_fusion.4), custom_call_target="InvertDiagBlocksLowerTriangular" | custom-call | tf_op jit(solution)/shard_map/jvp(vmap())/while/body/eval_jaxpr/jit(_solve_triangular)/triangular_solve/custom-call.1 | solution.py:57
  554.7 1.8 bitcast_dynamic-update-slice_fusion.22
  557.9 1.7 bitcast_dynamic-update-slice_fusion.24
  569.3 127.3 %while.165 = (s32[]{:T(128)}, f32[2,128,128]{2,1,0:T(8,128)S(1)}, f32[4,2,64,128]{3,2,1,0:T(8,128)}, f32[4,2,64,128]{3,2,1,0:T(8,128)}, f32[4,2,64,128]{3,2,0,1:...) while((s32[]{:T(128)}, f32[2,128,128]{2,1,0:T(8,128)S(1)}, ...), condition=%wide.region_25.27_spmd.clone.clone, body=%wide.region_14.26_spmd.clone.clone.sunk | while | flops 283857920 | bytes 5617773 | solution.py:86
  572.9 9.8 %custom-call.34 = f32[2,1,64,64]{2,3,1,0:T(8,128)S(1)} custom-call(f32[2,1,64,64]{3,2,1,0:T(8,128)S(1)} %select_bitcast_fusion.5), custom_call_target="InvertDiagBlocksLowerTriangular" | custom-call | tf_op jit(solution)/shard_map/transpose(jvp(vmap()))/while/body/eval_jaxpr/jit(_solve_triangular)/triangular_solve | solution.py:57
  591.1 1.7 fusion.375
  594.8 1.8 fusion.380
  604.8 9.8 %custom-call.34 = f32[2,1,64,64]{2,3,1,0:T(8,128)S(1)} custom-call(f32[2,1,64,64]{3,2,1,0:T(8,128)S(1)} %select_bitcast_fusion.5), custom_call_target="InvertDiagBlocksLowerTriangular" | custom-call | tf_op jit(solution)/shard_map/transpose(jvp(vmap()))/while/body/eval_jaxpr/jit(_solve_triangular)/triangular_solve | solution.py:57
  622.9 1.7 fusion.375
  626.6 1.8 fusion.380
  636.6 9.8 %custom-call.34 = f32[2,1,64,64]{2,3,1,0:T(8,128)S(1)} custom-call(f32[2,1,64,64]{3,2,1,0:T(8,128)S(1)} %select_bitcast_fusion.5), custom_call_target="InvertDiagBlocksLowerTriangular" | custom-call | tf_op jit(solution)/shard_map/transpose(jvp(vmap()))/while/body/eval_jaxpr/jit(_solve_triangular)/triangular_solve | solution.py:57
  654.8 1.7 fusion.375
  658.5 1.8 fusion.380
  668.4 9.8 %custom-call.34 = f32[2,1,64,64]{2,3,1,0:T(8,128)S(1)} custom-call(f32[2,1,64,64]{3,2,1,0:T(8,128)S(1)} %select_bitcast_fusion.5), custom_call_target="InvertDiagBlocksLowerTriangular" | custom-call | tf_op jit(solution)/shard_map/transpose(jvp(vmap()))/while/body/eval_jaxpr/jit(_solve_triangular)/triangular_solve | solution.py:57
  686.6 1.7 fusion.375
  690.3 1.8 fusion.380
  701.7 1.5 multiply_reduce_fusion.3
  705.2 1.4 collective-permute-done.1
  707.4 12.7 %all-to-all-start.1 = ((bf16[16,16,512]{2,1,0:T(8,128)(2,1)}), bf16[16,16,512]{2,1,0:T(8,128)(2,1)S(1)}, u32[]{:S(2)}, u32[]{:S(2)}) async-start(bf16[16,16,512]{2,1,0:T(8,128)(2,1)} %bitcast.32), calls=%async_computation.1 | async-start | bytes 524288 | tf_op jit(solution)/shard_map/all_to_all | solution.py:170
  720.8 66.5 %psum.7 = f32[4,512]{1,0:T(4,128)} all-reduce(f32[4,512]{1,0:T(4,128)S(1)} %pad_add_fusion.5), channel_id=1, replica_groups=mesh['ctx'=32,'head'=16] {'ctx'}, use_global_device_ids=true, to_apply=%region_34.36 | all-reduce | flops 2048 | bytes 16384 | tf_op jit(solution)/shard_map/psum | solution.py:173
  (724 shorter events, 346.5 us)
Async XLA Ops:
  7.2 438.4 %copy-start = (f32[2,128,128]{2,1,0:T(8,128)S(1)}, f32[2,128,128]{2,1,0:T(8,128)}, u32[]{:S(2)}) copy-start(f32[2,128,128]{2,1,0:T(8,128)} %param.25) | copy-start | bytes 393220
  8.9 33.1 %all-to-all-start = ((bf16[16,16,512]{2,0,1:T(8,128)(2,1)}), bf16[16,16,512]{2,0,1:T(8,128)(2,1)S(1)}, u32[]{:S(2)}, u32[]{:S(2)}) async-start(bf16[16,16,512]{2,0,1:T(8,128)(2,1)} %bitcast.435), calls=%async_computation | async-start | bytes 524288 | tf_op jit(solution)/shard_map/all_to_all | solution.py:138
  24.1 149.1 %all-gather.9.cloned.1.call-start = ((), (), s32[]{:S(2)}) async-start(), calls=%async_computation.2 | async-start | bytes 4325376 | tf_op jit(solution)/shard_map/all_gather | solution.py:24
  26.3 21.4 %copy-start.8 = (f32[1,512]{1,0:T(1,128)}, f32[1,512]{1,0:T(1,128)S(1)}, u32[]{:S(2)}) copy-start(f32[1,512]{1,0:T(1,128)S(1)} %get-tuple-element.3118) | copy-start | bytes 6148
  26.3 21.4 %copy-start.10 = (f32[1,512]{1,0:T(1,128)}, f32[1,512]{1,0:T(1,128)S(1)}, u32[]{:S(2)}) copy-start(f32[1,512]{1,0:T(1,128)S(1)} %get-tuple-element.3119) | copy-start | bytes 6148
  26.3 21.4 %copy-start.12 = (f32[1,512]{1,0:T(1,128)}, f32[1,512]{1,0:T(1,128)S(1)}, u32[]{:S(2)}) copy-start(f32[1,512]{1,0:T(1,128)S(1)} %get-tuple-element.3120) | copy-start | bytes 6148
  26.4 21.4 %copy-start.14 = (f32[1,512]{1,0:T(1,128)}, f32[1,512]{1,0:T(1,128)S(1)}, u32[]{:S(2)}) copy-start(f32[1,512]{1,0:T(1,128)S(1)} %get-tuple-element.3121) | copy-start | bytes 6148
  42.0 3.4 collective-permute-start
  46.7 0.6 copy-start.18
  46.7 1.8 copy-start.19
  47.3 1.3 copy-start.17
  48.5 66.4 %copy-start.5 = (bf16[256,256]{1,0:T(8,128)(2,1)S(1)}, bf16[256,256]{1,0:T(8,128)(2,1)}, u32[]{:S(2)}) copy-start(bf16[256,256]{1,0:T(8,128)(2,1)} %param.27) | copy-start | bytes 393220
  114.1 2.8 copy-start.2
  114.1 2.8 copy-start.3
  114.9 123.0 %all-gather.11.cloned.1.call-start = ((), (), s32[]{:S(2)}) async-start(), calls=%async_computation.3 | async-start | bytes 4325376 | tf_op jit(solution)/shard_map/all_gather | solution.py:24
  126.2 0.7 copy-start.1
  126.8 191.2 %all-gather.13.cloned.1.call-start = ((), (), s32[]{:S(2)}) async-start(), calls=%async_computation.4 | async-start | bytes 4325376 | tf_op jit(solution)/shard_map/all_gather | solution.py:24
  127.6 238.3 %all-gather.15.cloned.1.call-start = ((), (), s32[]{:S(2)}) async-start(), calls=%async_computation.5 | async-start | bytes 4325376 | tf_op jit(solution)/shard_map/all_gather | solution.py:24
  318.0 47.9 %copy-start.4 = (f32[2,128,128]{2,1,0:T(8,128)}, f32[2,128,128]{2,1,0:T(8,128)S(1)}, u32[]{:S(2)}) copy-start(f32[2,128,128]{2,1,0:T(8,128)S(1)} %get-tuple-element.2004) | copy-start | bytes 393220
  569.3 29.8 %copy-start.7 = (f32[4,2,64]{2,1,0:T(2,128)S(1)}, f32[4,2,64]{2,1,0:T(2,128)}, u32[]{:S(2)}) copy-start(f32[4,2,64]{2,1,0:T(2,128)} %get-tuple-element.4201) | copy-start | bytes 6148 | tf_op jit(solution)/shard_map/transpose(jvp(vmap()))/while
  569.3 30.1 %copy-start.6 = (f32[4,2,64]{2,1,0:T(2,128)S(1)}, f32[4,2,64]{2,1,0:T(2,128)}, u32[]{:S(2)}) copy-start(f32[4,2,64]{2,1,0:T(2,128)} %get-tuple-element.4198) | copy-start | bytes 6148 | tf_op jit(solution)/shard_map/transpose(jvp(vmap()))/while
  601.2 29.8 %copy-start.7 = (f32[4,2,64]{2,1,0:T(2,128)S(1)}, f32[4,2,64]{2,1,0:T(2,128)}, u32[]{:S(2)}) copy-start(f32[4,2,64]{2,1,0:T(2,128)} %get-tuple-element.4201) | copy-start | bytes 6148 | tf_op jit(solution)/shard_map/transpose(jvp(vmap()))/while
  601.2 30.0 %copy-start.6 = (f32[4,2,64]{2,1,0:T(2,128)S(1)}, f32[4,2,64]{2,1,0:T(2,128)}, u32[]{:S(2)}) copy-start(f32[4,2,64]{2,1,0:T(2,128)} %get-tuple-element.4198) | copy-start | bytes 6148 | tf_op jit(solution)/shard_map/transpose(jvp(vmap()))/while
  633.0 29.8 %copy-start.7 = (f32[4,2,64]{2,1,0:T(2,128)S(1)}, f32[4,2,64]{2,1,0:T(2,128)}, u32[]{:S(2)}) copy-start(f32[4,2,64]{2,1,0:T(2,128)} %get-tuple-element.4201) | copy-start | bytes 6148 | tf_op jit(solution)/shard_map/transpose(jvp(vmap()))/while
  633.0 30.0 %copy-start.6 = (f32[4,2,64]{2,1,0:T(2,128)S(1)}, f32[4,2,64]{2,1,0:T(2,128)}, u32[]{:S(2)}) copy-start(f32[4,2,64]{2,1,0:T(2,128)} %get-tuple-element.4198) | copy-start | bytes 6148 | tf_op jit(solution)/shard_map/transpose(jvp(vmap()))/while
  664.8 29.8 %copy-start.7 = (f32[4,2,64]{2,1,0:T(2,128)S(1)}, f32[4,2,64]{2,1,0:T(2,128)}, u32[]{:S(2)}) copy-start(f32[4,2,64]{2,1,0:T(2,128)} %get-tuple-element.4201) | copy-start | bytes 6148 | tf_op jit(solution)/shard_map/transpose(jvp(vmap()))/while
  664.8 30.1 %copy-start.6 = (f32[4,2,64]{2,1,0:T(2,128)S(1)}, f32[4,2,64]{2,1,0:T(2,128)}, u32[]{:S(2)}) copy-start(f32[4,2,64]{2,1,0:T(2,128)} %get-tuple-element.4198) | copy-start | bytes 6148 | tf_op jit(solution)/shard_map/transpose(jvp(vmap()))/while
  696.7 6.5 copy-start.9
  696.7 6.6 copy-start.11
  696.7 6.6 copy-start.13
  696.7 6.6 copy-start.15
  703.5 16.6 %copy-start.16 = (f32[4,2,64]{2,1,0:T(2,128)S(1)}, f32[4,2,64]{2,1,0:T(2,128)}, u32[]{:S(2)}) copy-start(f32[4,2,64]{2,1,0:T(2,128)} %get-tuple-element.2034) | copy-start | bytes 6148
  703.5 83.7 %copy-start.20 = (f32[2,256]{1,0:T(2,128)S(1)}, f32[2,256]{1,0:T(2,128)}, u32[]{:S(2)}) copy-start(f32[2,256]{1,0:T(2,128)} %param.23) | copy-start | bytes 6148
  703.6 3.1 collective-permute-start.1
  707.4 80.5 %all-to-all-start.1 = ((bf16[16,16,512]{2,1,0:T(8,128)(2,1)}), bf16[16,16,512]{2,1,0:T(8,128)(2,1)S(1)}, u32[]{:S(2)}, u32[]{:S(2)}) async-start(bf16[16,16,512]{2,1,0:T(8,128)(2,1)} %bitcast.32), calls=%async_computation.1 | async-start | bytes 524288 | tf_op jit(solution)/shard_map/all_to_all | solution.py:170
Sparse Core Ops, SparseCore 0:
  115.0 58.1 all-gather.8
  176.9 60.8 all-gather.10
  241.0 60.9 all-gather.12
  304.9 60.8 all-gather.14
where the time goes:
time: 802 us; the launch traced here: 795 us
  matrix products  258 us (32%)
  other arithmetic  180 us (22%)
  waiting for transfers between devices  176 us (22%)
  blocking collectives  66.5 us (8%)
  local copies, waits for them, and re-layouts  64.8 us (8%)
  starting transfers between devices  30.8 us (4%)
  between operations  14.3 us (2%)
    all_gather x4, waiting for transfers between devices, prefix(): everything = jax.tree.map(lambda part: lax.all_gather(part, axis), value)  158 us
    another operation x32, other arithmetic, block_step(): solved = jax.scipy.linalg.solve_triangular(system, right_sides, lower=True)  133 us
    dot_general x64, matrix products, compose(): jnp.einsum('hij,hjk->hik', later[0], earlier[1], precision=highest)  79.3 us
    dot_general x64, matrix products, compose(): matrix = jnp.einsum('hij,hjk->hik', later[0], earlier[0], precision=highest)  75.2 us
    psum x1, blocking collectives, on_device(): weight_total = lax.psum(grad_weight, 'ctx')  66.5 us
    dynamic_update_slice x24, other arithmetic, run_head(): (state_end, transit), outputs = lax.scan(block_step, start, pieces)  18.8 us
    dot_general x16, matrix products, block_step(): scores = ratios * jnp.dot(queries, key_feats.T, precision=highest)  18.5 us
    dot_general x20, matrix products, block_step(): jnp.dot(tail_keys.T, update, precision=highest)  17.8 us
  transfers between devices with their start and end apart: 8, of which 5 were waited for; matrix products, arithmetic and copies ran while one was open for 12% of the time, Pallas kernels for 0%

commit v1 on v0

--- a/solution.py
+++ b/solution.py
@@ -11,6 +11,13 @@
 BLOCK = 64
 highest = lax.Precision.HIGHEST
 norm_eps = 1e-06
+
+
+def swap_blocks(x, name, split, join):
+    size = lax.axis_size(name)
+    pieces = jnp.stack(jnp.split(x, size, axis=split), axis=0)
+    pieces = lax.all_to_all(pieces, name, split_axis=0, concat_axis=0)
+    return jnp.concatenate(pieces, axis=join)
 
 
 def from_behind(value, axis, by):
@@ -135,7 +142,7 @@
     final_state_grad,
     grad_out,
 ):
-    local_in = lax.all_to_all(mixed_in, "head", split_axis=1, concat_axis=0, tiled=True)
+    local_in = swap_blocks(mixed_in, "head", 1, 0)
     edge_rows = from_behind(local_in[-(KW - 1) :], "ctx", 1)
     extended = jnp.concatenate([edge_rows, local_in], axis=0).astype(jnp.float32)
     cotangent = grad_out.astype(jnp.float32)

time: 802 us -> 819 us (1.021)
  local copies, waits for them, and re-layouts: 64.8 us -> 85.1 us
    unnamed x42 -> x55, local copies, waits for them, and re-layouts: 2.93 us -> 24.4 us
where the time goes in v1:
time: 819 us; the launch traced here: 812 us
  matrix products  255 us (31%)
  other arithmetic  178 us (22%)
  waiting for transfers between devices  177 us (22%)
  local copies, waits for them, and re-layouts  85.1 us (10%)
  blocking collectives  66.4 us (8%)
  starting transfers between devices  30.8 us (4%)
  between operations  14.4 us (2%)
    all_gather x4, waiting for transfers between devices, prefix(): everything = jax.tree.map(lambda part: lax.all_gather(part, axis), value)  158 us
    another operation x32, other arithmetic, block_step(): solved = jax.scipy.linalg.solve_triangular(system, right_sides, lower=True)  133 us
    dot_general x64, matrix products, compose(): jnp.einsum('hij,hjk->hik', later[0], earlier[1], precision=highest)  79.3 us
    dot_general x64, matrix products, compose(): matrix = jnp.einsum('hij,hjk->hik', later[0], earlier[0], precision=highest)  75.3 us
    psum x1, blocking collectives, on_device(): weight_total = lax.psum(grad_weight, 'ctx')  66.4 us
    unnamed x55, local copies, waits for them, and re-layouts  24.4 us
    dot_general x16, matrix products, block_step(): scores = ratios * jnp.dot(queries, key_feats.T, precision=highest)  18.5 us
  transfers between devices with their start and end apart: 8, of which 5 were waited for; matrix products, arithmetic and copies ran while one was open for 12% of the time, Pallas kernels for 0%

profile of v1, /device:TPU:32, one launch (start us, length us, event | category | flops | bytes accessed | tf_op | source)
XLA Modules:
  0.0 811.5 jit_solution(10520390269512810290)
XLA Ops:
  28.4 15.2 %all-to-all-start = ((bf16[16,16,512]{2,1,0:T(8,128)(2,1)}), bf16[16,16,512]{2,1,0:T(8,128)(2,1)S(1)}, u32[]{:S(2)}, u32[]{:S(2)}) async-start(bf16[16,16,512]{2,1,0:T(8,128)(2,1)} %constant_dynamic-update-slice_fusion.11), calls=%async_computation | async-start | bytes 524288 | tf_op jit(solution)/shard_map/all_to_all | solution.py:19
  45.9 15.6 %all-to-all-done = bf16[16,16,512]{2,1,0:T(8,128)(2,1)S(1)} async-done(((bf16[16,16,512]{2,1,0:T(8,128)(2,1)}), bf16[16,16,512]{2,1,0:T(8,128)(2,1)S(1)}, u32[]{:S(2)}, u32[]{:S(2)}) %all-to-all-start) | async-done | bytes 262176 | tf_op jit(solution)/shard_map/all_to_all | solution.py:19
  67.4 63.1 %while.169 = (s32[]{:T(128)}, f32[2,128,128]{2,1,0:T(8,128)S(1)}, f32[2,128,128]{2,1,0:T(8,128)S(1)}, f32[4,2,64,128]{3,2,1,0:T(8,128)S(1)}, f32[4,2,64,1]{2,1,3...) while((s32[]{:T(128)}, f32[2,128,128]{2,1,0:T(8,128)S(1)}, ...), condition=%wide.region_4.6_spmd.clone.clone, body=%wide.region_2.5_spmd.clone.clone.sunk | while | flops 176640128 | bytes 2981140 | solution.py:93
  70.4 9.8 %custom-call.37 = f32[2,1,64,64]{2,3,1,0:T(8,128)S(1)} custom-call(f32[2,1,64,64]{3,2,1,0:T(8,128)S(1)} %fusion.420), custom_call_target="InvertDiagBlocksLowerTriangular" | custom-call | tf_op jit(solution)/shard_map/jvp(vmap())/while/body/eval_jaxpr/jit(_solve_triangular)/triangular_solve/custom-call.1 | solution.py:64
  86.1 9.8 %custom-call.37 = f32[2,1,64,64]{2,3,1,0:T(8,128)S(1)} custom-call(f32[2,1,64,64]{3,2,1,0:T(8,128)S(1)} %fusion.420), custom_call_target="InvertDiagBlocksLowerTriangular" | custom-call | tf_op jit(solution)/shard_map/jvp(vmap())/while/body/eval_jaxpr/jit(_solve_triangular)/triangular_solve/custom-call.1 | solution.py:64
  101.9 9.8 %custom-call.37 = f32[2,1,64,64]{2,3,1,0:T(8,128)S(1)} custom-call(f32[2,1,64,64]{3,2,1,0:T(8,128)S(1)} %fusion.420), custom_call_target="InvertDiagBlocksLowerTriangular" | custom-call | tf_op jit(solution)/shard_map/jvp(vmap())/while/body/eval_jaxpr/jit(_solve_triangular)/triangular_solve/custom-call.1 | solution.py:64
  117.7 9.8 %custom-call.37 = f32[2,1,64,64]{2,3,1,0:T(8,128)S(1)} custom-call(f32[2,1,64,64]{3,2,1,0:T(8,128)S(1)} %fusion.420), custom_call_target="InvertDiagBlocksLowerTriangular" | custom-call | tf_op jit(solution)/shard_map/jvp(vmap())/while/body/eval_jaxpr/jit(_solve_triangular)/triangular_solve/custom-call.1 | solution.py:64
  131.4 1.7 copy.129
  135.8 5.9 while.166
  143.7 46.0 %all-gather.9.cloned.1.call-done = f32[64,128,128]{2,1,0:T(8,128)} async-done(((f32[2,128,128]{2,1,0:T(8,128)}), f32[64,128,128]{2,1,0:T(8,128)}) %all-gather.9.cloned.1.call-update) | async-done | bytes 4194320 | tf_op jit(solution)/shard_map/all_gather | solution.py:31
  189.7 64.6 %all-gather.11.cloned.1.call-done = f32[64,128,128]{2,1,0:T(8,128)} async-done(((f32[2,128,128]{2,1,0:T(8,128)}), f32[64,128,128]{2,1,0:T(8,128)}) %all-gather.11.cloned.1.call-update) | async-done | bytes 4194320 | tf_op jit(solution)/shard_map/all_gather | solution.py:31
  254.3 80.1 %while.167 = (s32[]{:T(128)}, f32[2,128,128]{2,1,0:T(8,128)S(1)}, f32[2,128,128]{2,1,0:T(8,128)S(1)}, s32[]{:T(128)}, f32[32,2,128,128]{3,2,1,0:T(8,128)}, /*ind...) while((s32[]{:T(128)}, f32[2,128,128]{2,1,0:T(8,128)S(1)}, ...), condition=%wide.region_8.10_spmd.clone, body=%wide.region_7.9_spmd.clone.sunk | while | flops 100827144 | bytes 1706674 | solution.py:44
  334.5 47.8 %all-gather.15.cloned.1.call-done = f32[64,128,128]{2,1,0:T(8,128)} async-done(((f32[2,128,128]{2,1,0:T(8,128)}), f32[64,128,128]{2,1,0:T(8,128)}) %all-gather.15.cloned.1.call-update) | async-done | bytes 4194320 | tf_op jit(solution)/shard_map/all_gather | solution.py:31
  382.4 79.7 %while.168 = (s32[]{:T(128)}, f32[2,128,128]{2,1,0:T(8,128)S(1)}, f32[2,128,128]{2,1,0:T(8,128)S(1)}, s32[]{:T(128)}, f32[32,2,128,128]{3,2,1,0:T(8,128)}, /*ind...) while((s32[]{:T(128)}, f32[2,128,128]{2,1,0:T(8,128)S(1)}, f32[2,128,128]{2,1,0:T(8,128)S(1)}, ...), condition=%wide.region_10.12_spmd.clone, body=%wide.region_9.11_spmd.clone.sunk | while | flops 100827136 | bytes 1706612 | solution.py:44
  474.5 107.3 %while.164 = (s32[]{:T(128)}, f32[2,128,128]{2,1,0:T(8,128)S(1)}, f32[4,2,64,64]{3,2,1,0:T(8,128)}, f32[4,2,128,64]{2,3,1,0:T(8,128)}, f32[4,2,64,64]{3,2,1,0:T(...) while((s32[]{:T(128)}, f32[2,128,128]{2,1,0:T(8,128)S(1)}, ...), condition=%wide.region_13.15_spmd.clone.clone, body=%wide.region_11.14_spmd.clone.clone.sunk | while | flops 126194176 | bytes 3312057 | solution.py:93
  478.1 1.4 select_bitcast_fusion.4
  479.6 11.2 %custom-call.35 = f32[2,1,64,64]{2,3,1,0:T(8,128)} custom-call(f32[2,1,64,64]{3,2,1,0:T(8,128)} %select_bitcast_fusion.4), custom_call_target="InvertDiagBlocksLowerTriangular" | custom-call | tf_op jit(solution)/shard_map/jvp(vmap())/while/body/eval_jaxpr/jit(_solve_triangular)/triangular_solve/custom-call.1 | solution.py:64
  490.8 1.8 bitcast_dynamic-update-slice_fusion.22
  493.9 1.7 bitcast_dynamic-update-slice_fusion.24
  504.9 1.4 select_bitcast_fusion.4
  506.4 11.2 %custom-call.35 = f32[2,1,64,64]{2,3,1,0:T(8,128)} custom-call(f32[2,1,64,64]{3,2,1,0:T(8,128)} %select_bitcast_fusion.4), custom_call_target="InvertDiagBlocksLowerTriangular" | custom-call | tf_op jit(solution)/shard_map/jvp(vmap())/while/body/eval_jaxpr/jit(_solve_triangular)/triangular_solve/custom-call.1 | solution.py:64
  517.6 1.8 bitcast_dynamic-update-slice_fusion.22
  520.7 1.7 bitcast_dynamic-update-slice_fusion.24
  531.8 1.4 select_bitcast_fusion.4
  533.2 11.2 %custom-call.35 = f32[2,1,64,64]{2,3,1,0:T(8,128)} custom-call(f32[2,1,64,64]{3,2,1,0:T(8,128)} %select_bitcast_fusion.4), custom_call_target="InvertDiagBlocksLowerTriangular" | custom-call | tf_op jit(solution)/shard_map/jvp(vmap())/while/body/eval_jaxpr/jit(_solve_triangular)/triangular_solve/custom-call.1 | solution.py:64
  544.4 1.8 bitcast_dynamic-update-slice_fusion.22
  547.5 1.7 bitcast_dynamic-update-slice_fusion.24
  558.6 1.4 select_bitcast_fusion.4
  560.0 11.2 %custom-call.35 = f32[2,1,64,64]{2,3,1,0:T(8,128)} custom-call(f32[2,1,64,64]{3,2,1,0:T(8,128)} %select_bitcast_fusion.4), custom_call_target="InvertDiagBlocksLowerTriangular" | custom-call | tf_op jit(solution)/shard_map/jvp(vmap())/while/body/eval_jaxpr/jit(_solve_triangular)/triangular_solve/custom-call.1 | solution.py:64
  571.2 1.8 bitcast_dynamic-update-slice_fusion.22
  574.4 1.7 bitcast_dynamic-update-slice_fusion.24
  585.9 127.4 %while.165 = (s32[]{:T(128)}, f32[2,128,128]{2,1,0:T(8,128)S(1)}, f32[4,2,64,128]{3,2,1,0:T(8,128)}, f32[4,2,64,128]{3,2,1,0:T(8,128)}, f32[4,2,64,128]{3,2,0,1:...) while((s32[]{:T(128)}, f32[2,128,128]{2,1,0:T(8,128)S(1)}, ...), condition=%wide.region_25.27_spmd.clone.clone, body=%wide.region_14.26_spmd.clone.clone.sunk | while | flops 283857920 | bytes 5617773 | solution.py:93
  589.5 9.8 %custom-call.36 = f32[2,1,64,64]{2,3,1,0:T(8,128)S(1)} custom-call(f32[2,1,64,64]{3,2,1,0:T(8,128)S(1)} %select_bitcast_fusion.5), custom_call_target="InvertDiagBlocksLowerTriangular" | custom-call | tf_op jit(solution)/shard_map/transpose(jvp(vmap()))/while/body/eval_jaxpr/jit(_solve_triangular)/triangular_solve | solution.py:64
  607.6 1.7 fusion.375
  611.3 1.8 fusion.380
  621.3 9.8 %custom-call.36 = f32[2,1,64,64]{2,3,1,0:T(8,128)S(1)} custom-call(f32[2,1,64,64]{3,2,1,0:T(8,128)S(1)} %select_bitcast_fusion.5), custom_call_target="InvertDiagBlocksLowerTriangular" | custom-call | tf_op jit(solution)/shard_map/transpose(jvp(vmap()))/while/body/eval_jaxpr/jit(_solve_triangular)/triangular_solve | solution.py:64
  639.5 1.7 fusion.375
  643.2 1.8 fusion.380
  653.2 9.8 %custom-call.36 = f32[2,1,64,64]{2,3,1,0:T(8,128)S(1)} custom-call(f32[2,1,64,64]{3,2,1,0:T(8,128)S(1)} %select_bitcast_fusion.5), custom_call_target="InvertDiagBlocksLowerTriangular" | custom-call | tf_op jit(solution)/shard_map/transpose(jvp(vmap()))/while/body/eval_jaxpr/jit(_solve_triangular)/triangular_solve | solution.py:64
  671.3 1.7 fusion.375
  675.0 1.8 fusion.380
  685.0 9.8 %custom-call.36 = f32[2,1,64,64]{2,3,1,0:T(8,128)S(1)} custom-call(f32[2,1,64,64]{3,2,1,0:T(8,128)S(1)} %select_bitcast_fusion.5), custom_call_target="InvertDiagBlocksLowerTriangular" | custom-call | tf_op jit(solution)/shard_map/transpose(jvp(vmap()))/while/body/eval_jaxpr/jit(_solve_triangular)/triangular_solve | solution.py:64
  703.1 1.7 fusion.375
  706.8 1.8 fusion.380
  718.1 1.5 multiply_reduce_fusion.3
  721.6 1.4 collective-permute-done.1
  723.8 12.7 %all-to-all-start.1 = ((bf16[16,16,512]{2,1,0:T(8,128)(2,1)}), bf16[16,16,512]{2,1,0:T(8,128)(2,1)S(1)}, u32[]{:S(2)}, u32[]{:S(2)}) async-start(bf16[16,16,512]{2,1,0:T(8,128)(2,1)} %bitcast.48), calls=%async_computation.1 | async-start | bytes 524288 | tf_op jit(solution)/shard_map/all_to_all | solution.py:177
  737.2 66.4 %psum.7 = f32[4,512]{1,0:T(4,128)} all-reduce(f32[4,512]{1,0:T(4,128)S(1)} %pad_add_fusion.5), channel_id=1, replica_groups=mesh['ctx'=32,'head'=16] {'ctx'}, use_global_device_ids=true, to_apply=%region_34.36 | all-reduce | flops 2048 | bytes 16384 | tf_op jit(solution)/shard_map/psum | solution.py:180
  (737 shorter events, 361.9 us)
Async XLA Ops:
  7.2 454.9 %copy-start = (f32[2,128,128]{2,1,0:T(8,128)S(1)}, f32[2,128,128]{2,1,0:T(8,128)}, u32[]{:S(2)}) copy-start(f32[2,128,128]{2,1,0:T(8,128)} %param.25) | copy-start | bytes 393220
  28.4 33.1 %all-to-all-start = ((bf16[16,16,512]{2,1,0:T(8,128)(2,1)}), bf16[16,16,512]{2,1,0:T(8,128)(2,1)S(1)}, u32[]{:S(2)}, u32[]{:S(2)}) async-start(bf16[16,16,512]{2,1,0:T(8,128)(2,1)} %constant_dynamic-update-slice_fusion.11), calls=%async_computation | async-start | bytes 524288 | tf_op jit(solution)/shard_map/all_to_all | solution.py:19
  43.6 146.1 %all-gather.9.cloned.1.call-start = ((), (), s32[]{:S(2)}) async-start(), calls=%async_computation.2 | async-start | bytes 4325376 | tf_op jit(solution)/shard_map/all_gather | solution.py:31
  45.8 21.5 %copy-start.7 = (f32[1,512]{1,0:T(1,128)}, f32[1,512]{1,0:T(1,128)S(1)}, u32[]{:S(2)}) copy-start(f32[1,512]{1,0:T(1,128)S(1)} %get-tuple-element.3216) | copy-start | bytes 6148
  45.8 21.5 %copy-start.9 = (f32[1,512]{1,0:T(1,128)}, f32[1,512]{1,0:T(1,128)S(1)}, u32[]{:S(2)}) copy-start(f32[1,512]{1,0:T(1,128)S(1)} %get-tuple-element.3217) | copy-start | bytes 6148
  45.8 21.5 %copy-start.11 = (f32[1,512]{1,0:T(1,128)}, f32[1,512]{1,0:T(1,128)S(1)}, u32[]{:S(2)}) copy-start(f32[1,512]{1,0:T(1,128)S(1)} %get-tuple-element.3218) | copy-start | bytes 6148
  45.8 21.5 %copy-start.13 = (f32[1,512]{1,0:T(1,128)}, f32[1,512]{1,0:T(1,128)S(1)}, u32[]{:S(2)}) copy-start(f32[1,512]{1,0:T(1,128)S(1)} %get-tuple-element.3219) | copy-start | bytes 6148
  61.5 3.4 collective-permute-start
  66.2 0.6 copy-start.17
  66.2 1.2 copy-start.18
  66.8 0.7 copy-start.16
  130.5 5.3 copy-start.2
  130.6 5.3 copy-start.3
  131.3 123.0 %all-gather.11.cloned.1.call-start = ((), (), s32[]{:S(2)}) async-start(), calls=%async_computation.3 | async-start | bytes 4325376 | tf_op jit(solution)/shard_map/all_gather | solution.py:31
  141.7 0.7 copy-start.1
  142.4 192.1 %all-gather.13.cloned.1.call-start = ((), (), s32[]{:S(2)}) async-start(), calls=%async_computation.4 | async-start | bytes 4325376 | tf_op jit(solution)/shard_map/all_gather | solution.py:31
  143.1 239.2 %all-gather.15.cloned.1.call-start = ((), (), s32[]{:S(2)}) async-start(), calls=%async_computation.5 | async-start | bytes 4325376 | tf_op jit(solution)/shard_map/all_gather | solution.py:31
  334.5 47.9 %copy-start.4 = (f32[2,128,128]{2,1,0:T(8,128)}, f32[2,128,128]{2,1,0:T(8,128)S(1)}, u32[]{:S(2)}) copy-start(f32[2,128,128]{2,1,0:T(8,128)S(1)} %get-tuple-element.2004) | copy-start | bytes 393220
  585.9 29.8 %copy-start.6 = (f32[4,2,64]{2,1,0:T(2,128)S(1)}, f32[4,2,64]{2,1,0:T(2,128)}, u32[]{:S(2)}) copy-start(f32[4,2,64]{2,1,0:T(2,128)} %get-tuple-element.4299) | copy-start | bytes 6148 | tf_op jit(solution)/shard_map/transpose(jvp(vmap()))/while
  585.9 30.1 %copy-start.5 = (f32[4,2,64]{2,1,0:T(2,128)S(1)}, f32[4,2,64]{2,1,0:T(2,128)}, u32[]{:S(2)}) copy-start(f32[4,2,64]{2,1,0:T(2,128)} %get-tuple-element.4296) | copy-start | bytes 6148 | tf_op jit(solution)/shard_map/transpose(jvp(vmap()))/while
  617.7 29.8 %copy-start.6 = (f32[4,2,64]{2,1,0:T(2,128)S(1)}, f32[4,2,64]{2,1,0:T(2,128)}, u32[]{:S(2)}) copy-start(f32[4,2,64]{2,1,0:T(2,128)} %get-tuple-element.4299) | copy-start | bytes 6148 | tf_op jit(solution)/shard_map/transpose(jvp(vmap()))/while
  617.7 30.0 %copy-start.5 = (f32[4,2,64]{2,1,0:T(2,128)S(1)}, f32[4,2,64]{2,1,0:T(2,128)}, u32[]{:S(2)}) copy-start(f32[4,2,64]{2,1,0:T(2,128)} %get-tuple-element.4296) | copy-start | bytes 6148 | tf_op jit(solution)/shard_map/transpose(jvp(vmap()))/while
  649.6 29.8 %copy-start.6 = (f32[4,2,64]{2,1,0:T(2,128)S(1)}, f32[4,2,64]{2,1,0:T(2,128)}, u32[]{:S(2)}) copy-start(f32[4,2,64]{2,1,0:T(2,128)} %get-tuple-element.4299) | copy-start | bytes 6148 | tf_op jit(solution)/shard_map/transpose(jvp(vmap()))/while
  649.6 30.0 %copy-start.5 = (f32[4,2,64]{2,1,0:T(2,128)S(1)}, f32[4,2,64]{2,1,0:T(2,128)}, u32[]{:S(2)}) copy-start(f32[4,2,64]{2,1,0:T(2,128)} %get-tuple-element.4296) | copy-start | bytes 6148 | tf_op jit(solution)/shard_map/transpose(jvp(vmap()))/while
  681.4 29.8 %copy-start.6 = (f32[4,2,64]{2,1,0:T(2,128)S(1)}, f32[4,2,64]{2,1,0:T(2,128)}, u32[]{:S(2)}) copy-start(f32[4,2,64]{2,1,0:T(2,128)} %get-tuple-element.4299) | copy-start | bytes 6148 | tf_op jit(solution)/shard_map/transpose(jvp(vmap()))/while
  681.4 30.1 %copy-start.5 = (f32[4,2,64]{2,1,0:T(2,128)S(1)}, f32[4,2,64]{2,1,0:T(2,128)}, u32[]{:S(2)}) copy-start(f32[4,2,64]{2,1,0:T(2,128)} %get-tuple-element.4296) | copy-start | bytes 6148 | tf_op jit(solution)/shard_map/transpose(jvp(vmap()))/while
  713.2 6.4 copy-start.8
  713.2 6.4 copy-start.10
  713.2 6.4 copy-start.12
  713.2 6.4 copy-start.14
  719.9 16.6 %copy-start.15 = (f32[4,2,64]{2,1,0:T(2,128)S(1)}, f32[4,2,64]{2,1,0:T(2,128)}, u32[]{:S(2)}) copy-start(f32[4,2,64]{2,1,0:T(2,128)} %get-tuple-element.2034) | copy-start | bytes 6148
  720.0 83.7 %copy-start.19 = (f32[2,256]{1,0:T(2,128)S(1)}, f32[2,256]{1,0:T(2,128)}, u32[]{:S(2)}) copy-start(f32[2,256]{1,0:T(2,128)} %param.23) | copy-start | bytes 6148
  720.0 3.1 collective-permute-start.1
  723.8 80.5 %all-to-all-start.1 = ((bf16[16,16,512]{2,1,0:T(8,128)(2,1)}), bf16[16,16,512]{2,1,0:T(8,128)(2,1)S(1)}, u32[]{:S(2)}, u32[]{:S(2)}) async-start(bf16[16,16,512]{2,1,0:T(8,128)(2,1)} %bitcast.48), calls=%async_computation.1 | async-start | bytes 524288 | tf_op jit(solution)/shard_map/all_to_all | solution.py:177
Sparse Core Ops, SparseCore 0:
  131.5 58.1 all-gather.8
  193.4 60.8 all-gather.10
  257.4 60.9 all-gather.12
  321.4 60.8 all-gather.14
